TPU v7x, 32 devices: a whole 2x2x4 slice. The times are simulated.
32 devices in a mesh: grp: 2 (over x), tile: 8 (over z, y), freq: 2 (over core).
Axes of the slice: x: 2, y: 2, z: 4, core: 2. Of those that a mesh axis runs over, the one named last changes fastest.
Arguments:
- green_recv: bfloat16 [4, 2, 1024, 4096], P(('grp', 'freq'), None, None, 'tile'), parts along dimension 0, may hold values from -2 to 2
- green_shot: bfloat16 [4, 2, 512, 4096], P(('grp', 'freq'), None, None, 'tile'), parts along dimension 0, may hold values from -2.5 to 2.5
- band_mask: int32 [16, 5], P('grp'), parts along dimension 0, may hold values from 0 to 1, as said below
- live_counts: int32 [16], P('grp'), parts along dimension 0, may hold values from 128 to 512, as said below
- freq_bins: int32 [4], P(('grp', 'freq')), parts along dimension 0, may hold values from 256 to 511
Outputs:
- hessian: float32 [8192, 5, 512], P(('grp', 'tile', 'freq')), parts along dimension 0
There are 2 independent parts, one for each index of `grp`. A program takes and returns all parts, laid end to end along the dimension named above; each array names one. Nothing has to cross between parts.
Inputs may be any that keep to these rules, and one draw needn't show every extreme that they name: band_mask[t, 2 + d] equals band_mask[t + d, 2 - d], is 1 at d = 0, is 0 where t + d lies outside the tiles, and some tile has all 5 slots at 1. `live_counts`: some tile has all 512 points live.
All inputs are finite; a program needn't handle non-finite values.
Results may differ from a plain program's by a relative error of at most 0.00065.
Values may be sent and summed in bfloat16 or wider, within the bound.
A program may use at most 64 MiB of HBM per device.

v0:
```python
import jax
import jax.numpy as jnp
from jax import lax
from jax.sharding import PartitionSpec as P

BINS = 512


def from_behind(value, axis, steps):
    count = lax.axis_size(axis)
    initial, last = (max(0, -steps), min(count, count - steps))
    return lax.ppermute(value, axis, [(source, source + steps) for source in range(initial, last)])


def gram_pair(left_block, right_block):
    product = jnp.einsum(
        "fcri,fdrj->fcidj", left_block, right_block, preferred_element_type=jnp.float32
    )
    real_part = product[:, 0, :, 0] + product[:, 1, :, 1]
    imag_part = product[:, 1, :, 0] - product[:, 0, :, 1]
    return (real_part, imag_part)


def hadamard_sum(own_blocks, far_blocks, weights):
    recv_real, recv_imag = gram_pair(own_blocks[0], far_blocks[0])
    shot_real, shot_imag = gram_pair(own_blocks[1], far_blocks[1])
    return jnp.einsum(
        "f,fij->ij",
        weights,
        recv_real * shot_real - recv_imag * shot_imag,
        precision=lax.Precision.HIGHEST,
    )


def per_device(green_recv, green_shot, band_mask, live_counts, freq_bins):
    my_tile = lax.axis_index("tile")
    tile_count = lax.axis_size("tile")
    points = green_recv.shape[3]
    radius = band_mask.shape[1] // 2
    weights = (freq_bins.astype(jnp.float32) / BINS) ** 4
    indices = jnp.arange(points, dtype=jnp.int32)
    own_blocks = (green_recv, green_shot)
    live_own = (indices < live_counts[my_tile]).astype(jnp.float32)
    slot_row = band_mask[my_tile]

    def partner_block(far_blocks, offset):
        partner = my_tile + offset
        inside = (partner >= 0) & (partner < tile_count)
        clipped = jnp.clip(partner, 0, tile_count - 1)
        active = (slot_row[radius + offset] > 0) & inside
        live_far = (indices < live_counts[clipped]).astype(jnp.float32) * inside.astype(jnp.float32)
        summed = lax.cond(
            active,
            lambda: hadamard_sum(own_blocks, far_blocks, weights),
            lambda: jnp.zeros((points, points), jnp.float32),
        )
        return summed * live_own[:, None] * live_far[None, :]

    ahead_list = []
    behind = []
    self_block = partner_block(own_blocks, 0)
    for distance in range(1, radius + 1):
        far_blocks = from_behind((green_recv, green_shot), "tile", -distance)
        forward = partner_block(far_blocks, distance)
        mirrored = from_behind(forward.astype(jnp.bfloat16), "tile", distance).astype(forward.dtype)
        ahead_list.append(forward)
        behind.append(mirrored.T)
    blocks = behind[::-1] + [self_block] + ahead_list
    local_band = jnp.stack(blocks, axis=1)
    summed_band = lax.psum(local_band, "freq")
    half_rows = points // lax.axis_size("freq")
    return lax.dynamic_slice_in_dim(summed_band, lax.axis_index("freq") * half_rows, half_rows, 0)


def solution(mesh):
    return jax.shard_map(
        per_device,
        mesh=mesh,
        in_specs=(
            P(("grp", "freq"), None, None, "tile"),
            P(("grp", "freq"), None, None, "tile"),
            P("grp", None),
            P("grp"),
            P(("grp", "freq")),
        ),
        out_specs=P(("grp", "tile", "freq"), None, None),
        check_vma=False,
    )
```

profile of v0, /device:TPU:13, one launch (start us, length us, event | category | flops | bytes accessed | tf_op | source)
XLA Modules:
  0.0 234.8 jit_solution(7470893038034929075)
XLA Ops:
  6.5 0.0 copy-start
  6.5 0.0 all-reduce.2.cloned.1.call-start
  6.5 2.3 collective-permute-start.3
  8.8 1.9 collective-permute-start
  10.7 3.0 %collective-permute-start.4 = (bf16[1,2,512,512]{3,2,1,0:T(8,128)(2,1)}, bf16[1,2,512,512]{3,2,1,0:T(8,128)(2,1)S(1)}, u32[]{:S(2)}, u32[]{:S(2)}) collective-permute-start(bf16[1,2,512,512]{3,2,1,0:T(8,128)(2,1)} %param.12), channel_id=1, source_target_pairs={{2,0},{4,2},{6,4},{8,6},{10,8},{12,10},{14,12},{3,1},{5,3},{7,5},{... | collective-permute-start | bytes 3145736 | tf_op jit(solution)/shard_map/ppermute | solution.py:12
  13.8 1.9 collective-permute-start.1
  16.4 0.0 copy-done
  16.4 0.7 fusion.34
  18.3 1.5 fusion.33
  19.8 0.6 fusion.29
  20.4 1.3 fusion.30
  21.7 101.9 %collective-permute-done.4 = bf16[1,2,512,512]{3,2,1,0:T(8,128)(2,1)S(1)} collective-permute-done((bf16[1,2,512,512]{3,2,1,0:T(8,128)(2,1)}, bf16[1,2,512,512]{3,2,1,0:T(8,128)(2,1)S(1)}, u32[]{:S(2)}, u32[]{:S(2)}) %collective-permute-start.4) | collective-permute-done | bytes 1048608 | tf_op jit(solution)/shard_map/ppermute | solution.py:12
  123.6 0.0 collective-permute-done.3
  123.6 0.1 conditional.4
  123.6 0.1 broadcast.60
  123.7 0.0 collective-permute-done.1
  123.7 0.0 collective-permute-done
  123.7 0.1 conditional.3
  123.8 0.1 broadcast.59
  123.9 1.2 fusion.28
  125.1 33.1 %collective-permute-start.5 = (bf16[512,512]{1,0:T(8,128)(2,1)}, bf16[512,512]{1,0:T(8,128)(2,1)}, u32[]{:S(2)}, u32[]{:S(2)}) collective-permute-start(bf16[512,512]{1,0:T(8,128)(2,1)} %get-tuple-element.66), channel_id=1, source_target_pairs={{0,2},{2,4},{4,6},{6,8},{8,10},{10,12},{12,14},{1,3},{3,5},{5,7},{... | collective-permute-start | bytes 1572872 | tf_op jit(solution)/shard_map/ppermute | solution.py:12
  158.2 1.9 collective-permute-start.2
  160.9 6.7 %conditional.5 = (f32[512,512]{1,0:T(8,128)S(1)}) conditional(s32[]{:T(128)} %convert_element_type.47, () %tuple.27, (bf16[1,2,1024,512]{3,2,1,0:T(8,128)(2,1)}, bf16[1,2,512,512]{3,2,1,0:T(8,128)(2,1)}, f32[1]{0:T(128)}) %tuple.28), branch_computations={%region_4.5_spmd, %region_5.6_spmd} | conditional | flops 3223322624 | bytes 29360168 | solution.py:52
  161.1 0.0 copy-start.5
  161.1 3.0 %convolution_bitcast_fusion.4 = f32[1,2,512,2,512]{4,2,3,1,0:T(8,128)S(1)} fusion(bf16[1,2,512,512]{3,2,1,0:T(8,128)(2,1)} %get-tuple-element.64), kind=kOutput, calls=%fused_computation.30 | convolution fusion | flops 1073741824 | bytes 5242880 | tf_op jit(solution)/shard_map/cond/branch_1_fun/fcri,fdrj->fcidj/dot_general | solution.py:16
  164.1 0.0 copy-done.5
  164.1 2.4 %convolution_bitcast_fusion.5 = f32[1,2,512,2,512]{4,2,3,1,0:T(8,128)S(1)} fusion(bf16[1,2,1024,512]{3,2,1,0:T(8,128)(2,1)S(1)} %copy-done.5), kind=kOutput, calls=%fused_computation.31 | convolution fusion | flops 2147483648 | bytes 6291456 | tf_op jit(solution)/shard_map/cond/branch_1_fun/fcri,fdrj->fcidj/dot_general | solution.py:16
  166.5 1.0 fusion.23
  167.5 0.0 copy-start.1
  167.5 0.7 fusion.32
  168.2 0.1 collective-permute-done.5
  168.3 0.2 copy-done.1
  168.5 2.1 convert_bitcast_fusion
  170.7 1.6 copy.15
  172.2 8.2 %collective-permute-done.2 = bf16[512,512]{1,0:T(8,128)(2,1)} collective-permute-done((bf16[512,512]{1,0:T(8,128)(2,1)}, bf16[512,512]{1,0:T(8,128)(2,1)}, u32[]{:S(2)}, u32[]{:S(2)}) %collective-permute-start.2) | collective-permute-done | bytes 524320 | tf_op jit(solution)/shard_map/ppermute | solution.py:12
  180.4 2.1 convert_bitcast_fusion.1
  182.6 2.5 %copy.14 = f32[512,1,512]{2,0,1:T(8,128)} copy(f32[512,1,512]{0,2,1:T(8,128)} %convert_bitcast_fusion.1) | data formatting | bytes 2097152 | tf_op jit(solution)/shard_map/stack | solution.py:69
  185.1 0.0 copy-start.2
  185.1 2.4 %constant_dynamic-update-slice_fusion.1 = f32[512,5,512]{2,0,1:T(8,128)} fusion(f32[512,1,512]{2,0,1:T(8,128)} %copy.14), kind=kLoop, calls=%fused_computation.55 | loop fusion | bytes 2097152
  187.5 1.0 constant_dynamic-update-slice_fusion
  188.5 0.0 copy-done.2
  188.5 1.1 bitcast_dynamic-update-slice_fusion.2
  189.7 1.1 bitcast_dynamic-update-slice_fusion.1
  190.8 1.1 bitcast_dynamic-update-slice_fusion
  191.9 0.0 all-reduce.2.cloned.1.call-update
  192.0 32.3 %all-reduce.2.cloned.1.call-done = f32[512,5,512]{2,0,1:T(8,128)} async-done(((f32[512,5,512]{2,0,1:T(8,128)}), f32[512,5,512]{2,0,1:T(8,128)}) %all-reduce.2.cloned.1.call-update) | async-done | bytes 5242896 | tf_op jit(solution)/shard_map/psum | solution.py:70
  224.3 3.6 %constant_dynamic-slice_fusion = f32[256,5,512]{2,0,1:T(8,128)} fusion(f32[512,5,512]{2,0,1:T(8,128)} %all-reduce.2.cloned.1.call-done, s32[]{:T(128)S(6)} %select_n.5), kind=kLoop, calls=%fused_computation.64 | loop fusion | bytes 5242884 | tf_op jit(solution)/shard_map/dynamic_slice | solution.py:72
  (1 shorter events, 0.0 us)
Async XLA Ops:
  6.5 9.8 %copy-start = (s32[8,5]{1,0:T(8,128)S(1)}, s32[8,5]{1,0:T(8,128)}, u32[]{:S(2)}) copy-start(s32[8,5]{1,0:T(8,128)} %param.13) | copy-start | bytes 484
  6.5 217.8 %all-reduce.2.cloned.1.call-start = ((), (), s32[]{:S(2)}) async-start(), calls=%async_computation | async-start | bytes 10485760 | tf_op jit(solution)/shard_map/psum | solution.py:70
  6.5 117.1 %collective-permute-start.3 = (bf16[1,2,1024,512]{3,2,1,0:T(8,128)(2,1)}, bf16[1,2,1024,512]{3,2,1,0:T(8,128)(2,1)}, u32[]{:S(2)}, u32[]{:S(2)}) collective-permute-start(bf16[1,2,1024,512]{3,2,1,0:T(8,128)(2,1)} %param.11), channel_id=1, source_target_pairs={{2,0},{4,2},{6,4},{8,6},{10,8},{12,10},{14,12},{3,1},{5,3},{7,5},{... | collective-permute-start | bytes 6291464 | tf_op jit(solution)/shard_map/ppermute | solution.py:12
  8.8 114.9 %collective-permute-start = (bf16[1,2,1024,512]{3,2,1,0:T(8,128)(2,1)}, bf16[1,2,1024,512]{3,2,1,0:T(8,128)(2,1)}, u32[]{:S(2)}, u32[]{:S(2)}) collective-permute-start(bf16[1,2,1024,512]{3,2,1,0:T(8,128)(2,1)} %param.11), channel_id=1, source_target_pairs={{4,0},{6,2},{8,4},{10,6},{12,8},{14,10},{5,1},{7,3},{9,5},{11,7},{... | collective-permute-start | bytes 6291464 | tf_op jit(solution)/shard_map/ppermute | solution.py:12
  10.7 112.9 %collective-permute-start.4 = (bf16[1,2,512,512]{3,2,1,0:T(8,128)(2,1)}, bf16[1,2,512,512]{3,2,1,0:T(8,128)(2,1)S(1)}, u32[]{:S(2)}, u32[]{:S(2)}) collective-permute-start(bf16[1,2,512,512]{3,2,1,0:T(8,128)(2,1)} %param.12), channel_id=1, source_target_pairs={{2,0},{4,2},{6,4},{8,6},{10,8},{12,10},{14,12},{3,1},{5,3},{7,5},{... | collective-permute-start | bytes 3145736 | tf_op jit(solution)/shard_map/ppermute | solution.py:12
  13.8 110.0 %collective-permute-start.1 = (bf16[1,2,512,512]{3,2,1,0:T(8,128)(2,1)}, bf16[1,2,512,512]{3,2,1,0:T(8,128)(2,1)S(1)}, u32[]{:S(2)}, u32[]{:S(2)}) collective-permute-start(bf16[1,2,512,512]{3,2,1,0:T(8,128)(2,1)} %param.12), channel_id=1, source_target_pairs={{4,0},{6,2},{8,4},{10,6},{12,8},{14,10},{5,1},{7,3},{9,5},{11,7},{... | collective-permute-start | bytes 3145736 | tf_op jit(solution)/shard_map/ppermute | solution.py:12
  125.1 43.2 %collective-permute-start.5 = (bf16[512,512]{1,0:T(8,128)(2,1)}, bf16[512,512]{1,0:T(8,128)(2,1)}, u32[]{:S(2)}, u32[]{:S(2)}) collective-permute-start(bf16[512,512]{1,0:T(8,128)(2,1)} %get-tuple-element.66), channel_id=1, source_target_pairs={{0,2},{2,4},{4,6},{6,8},{8,10},{10,12},{12,14},{1,3},{3,5},{5,7},{... | collective-permute-start | bytes 1572872 | tf_op jit(solution)/shard_map/ppermute | solution.py:12
  158.2 22.2 %collective-permute-start.2 = (bf16[512,512]{1,0:T(8,128)(2,1)}, bf16[512,512]{1,0:T(8,128)(2,1)}, u32[]{:S(2)}, u32[]{:S(2)}) collective-permute-start(bf16[512,512]{1,0:T(8,128)(2,1)} %get-tuple-element.67), channel_id=1, source_target_pairs={{0,4},{2,6},{4,8},{6,10},{8,12},{10,14},{1,5},{3,7},{5,9},{7,11},{... | collective-permute-start | bytes 1572872 | tf_op jit(solution)/shard_map/ppermute | solution.py:12
  161.1 3.0 %copy-start.5 = (bf16[1,2,1024,512]{3,2,1,0:T(8,128)(2,1)S(1)}, bf16[1,2,1024,512]{3,2,1,0:T(8,128)(2,1)}, u32[]{:S(2)}) copy-start(bf16[1,2,1024,512]{3,2,1,0:T(8,128)(2,1)} %get-tuple-element.63) | copy-start | bytes 6291460 | tf_op jit(solution)/shard_map/cond
  167.5 1.0 copy-start.1
  185.1 3.4 %copy-start.2 = (f32[512,512]{1,0:T(8,128)S(1)}, f32[512,512]{1,0:T(8,128)}, u32[]{:S(2)}) copy-start(f32[512,512]{1,0:T(8,128)} %copy-done.1) | copy-start | bytes 3145732
Sparse Core Ops, SparseCore 0:
  192.1 32.1 all-reduce.1
where the time goes:
time: 236 us; the launch traced here: 235 us
  waiting for transfers between devices  143 us (61%)
  starting transfers between devices  44.2 us (19%)
  between operations  16.1 us (7%)
  local copies, waits for them, and re-layouts  13.8 us (6%)
  other arithmetic  12.5 us (5%)
  matrix products  5.39 us (2%)
    ppermute x6, waiting for transfers between devices, from_behind(): lax.ppermute(value, axis, [(source, source + steps) for source in range(i...  110 us
    ppermute x6, starting transfers between devices, from_behind(): lax.ppermute(value, axis, [(source, source + steps) for source in range(i...  44.2 us
    psum x1, waiting for transfers between devices, per_device(): summed_band = lax.psum(local_band, 'freq')  32.3 us
    another operation x3, other arithmetic, per_device(): local_band = jnp.stack(blocks, axis=1)  5.43 us
    dot_general x2, matrix products, gram_pair(): jnp.einsum('fcri,fdrj->fcidj', left_block, right_block, preferred_element...  5.39 us
  transfers between devices with their start and end apart: 7, of which 4 were waited for; matrix products, arithmetic and copies ran while one was open for 6% of the time, Pallas kernels for 0%

commit v1 on v0

v1 whole, which is shorter than its diff:
```python
import functools

import jax
import jax.numpy as jnp
from jax import lax
from jax.experimental import pallas as pl
from jax.experimental.pallas import tpu as pltpu
from jax.sharding import PartitionSpec as P

BINS = 512
MESH = pl.DeviceIdType.MESH
PAIRS = ((0, 1), (0, 2), (1, 2))
ROW = {1: 0, 2: 1, -1: 2, -2: 3}


def band_kernel(tiles, radius, recv_ref, shot_ref, band_ref, live_ref, bins_ref, out_ref,
                far_r, far_s, left_r, left_s, local, self_local, self_out, self_in, outbox, inbox,
                own_sem, data_send, data_recv, res_send, res_recv, self_send, self_recv):
    t = lax.axis_index("tile")
    f = lax.axis_index("freq")
    depth_r, points = recv_ref.shape
    depth_s = shot_ref.shape[0]
    half = points // 2
    step = 1 - 2 * f
    r = f * (tiles - 1) + step * t
    heavy = lax.rem(r, 2) == 0
    has_far = r + 2 < tiles
    weight_root = bins_ref[0].astype(jnp.float32) / BINS
    weight = (weight_root * weight_root) * (weight_root * weight_root)

    def columns(j):
        return pl.ds(pl.multiple_of(j * half, half), half)

    def own_copy(which, j):
        src, dst = ((recv_ref, far_r), (shot_ref, far_s))[which]
        return pltpu.make_async_copy(src.at[:, columns(j)], dst.at[0, j], own_sem.at[which, j])

    def data_copy(which, j, distance):
        src, dst = ((recv_ref, far_r), (shot_ref, far_s))[which]
        return pltpu.make_async_remote_copy(
            src_ref=src.at[:, columns(j)], dst_ref=dst.at[distance, j],
            send_sem=data_send.at[which, j, distance - 1], recv_sem=data_recv.at[which, j, distance - 1],
            device_id={"tile": t - step * distance}, device_id_type=MESH)

    for j in range(2):
        for which in range(2):
            own_copy(which, j).start()

    barrier = pltpu.get_barrier_semaphore()
    for distance in range(-2, 3):
        near = t + distance
        for turn in range(2):
            if distance == 0 and turn == 0:
                continue
            other = f if turn == 0 else 1 - f

            @pl.when((near >= 0) & (near < tiles))
            def _():
                pl.semaphore_signal(barrier, inc=1, device_id={"tile": near, "freq": other}, device_id_type=MESH)
    reached = jnp.minimum(t, 2) + jnp.minimum(tiles - 1 - t, 2)
    pl.semaphore_wait(barrier, 2 * reached + 1)

    for j in range(2):
        for which in range(2):
            @pl.when(jnp.logical_not(heavy))
            def _():
                data_copy(which, j, 1).start()

            @pl.when(r >= 2)
            def _():
                data_copy(which, j, 2).start()

    def build_left(slot, j):
        for src, dst, depth in ((far_r, left_r, depth_r // 2), (far_s, left_s, depth_s // 2)):
            part = min(depth, 512)

            @pl.loop(0, depth // part)
            def _(k):
                lo = pl.multiple_of(k * part, part)
                hi = pl.multiple_of(depth + k * part, part)
                re = src[slot, j, pl.ds(lo, part), :].T
                im = src[slot, j, pl.ds(hi, part), :].T
                dst[slot, j, 0:half, pl.ds(lo, part)] = re
                dst[slot, j, 0:half, pl.ds(hi, part)] = im
                dst[slot, j, half:points, pl.ds(lo, part)] = im
                dst[slot, j, half:points, pl.ds(hi, part)] = -re

    def block(slot, h, far, j):
        rr = jnp.dot(left_r[slot, h], far_r[far, j], preferred_element_type=jnp.float32)
        ss = jnp.dot(left_s[slot, h], far_s[far, j], preferred_element_type=jnp.float32)
        return (rr[:half] * ss[:half] - rr[half:] * ss[half:]) * weight

    def far_from(h):
        return jnp.where(h == f, 0, 1)

    def plain_send(k, h, j):
        first, second = PAIRS[k]
        return pltpu.make_async_remote_copy(
            src_ref=outbox.at[k, h, j, 0], dst_ref=inbox.at[far_from(h), ROW[second - first], j],
            send_sem=res_send.at[k, h, j, 0], recv_sem=res_recv.at[far_from(h), ROW[second - first], j],
            device_id={"tile": t + step * first, "freq": h}, device_id_type=MESH)

    def turned_send(k, h, j):
        first, second = PAIRS[k]
        return pltpu.make_async_remote_copy(
            src_ref=outbox.at[k, h, j, 1], dst_ref=inbox.at[far_from(j), ROW[first - second], h],
            send_sem=res_send.at[k, h, j, 1], recv_sem=res_recv.at[far_from(j), ROW[first - second], h],
            device_id={"tile": t + step * second, "freq": j}, device_id_type=MESH)

    def unit(k, h, j):
        first, second = PAIRS[k]
        value = block(first, h, second, j)
        outbox[k, h, j, 1] = value.T.astype(jnp.bfloat16)
        turned_send(k, h, j).start()
        if first == 0:
            @pl.when(h == f)
            def _():
                local[second - 1, j] = value

            @pl.when(h != f)
            def _():
                outbox[k, h, j, 0] = value.astype(jnp.bfloat16)
                plain_send(k, h, j).start()
        else:
            outbox[k, h, j, 0] = value.astype(jnp.bfloat16)
            plain_send(k, h, j).start()

    def self_copy(j):
        return pltpu.make_async_remote_copy(
            src_ref=self_out.at[j], dst_ref=self_in.at[j], send_sem=self_send.at[j], recv_sem=self_recv.at[j],
            device_id={"freq": 1 - f}, device_id_type=MESH)

    for j in range(2):
        for which in range(2):
            own_copy(which, j).wait()

    @pl.loop(0, 2)
    def _(j):
        build_left(0, j)

    @pl.loop(0, 2)
    def _(j):
        self_local[j] = block(0, f, 0, j)

    @pl.loop(0, 2)
    def _(j):
        self_out[j] = block(0, 1 - f, 0, j)
        self_copy(j).start()

    @pl.loop(0, 2)
    def _(j):
        @pl.when(heavy)
        def _():
            for which in range(2):
                data_copy(which, j, 1).wait_recv()

            @pl.loop(0, 2)
            def _(h):
                unit(0, h, j)

            build_left(1, j)

        @pl.when(has_far)
        def _():
            for which in range(2):
                data_copy(which, j, 2).wait_recv()

            @pl.loop(0, 2)
            def _(h):
                unit(1, h, j)

        @pl.when(heavy & has_far)
        def _():
            @pl.loop(0, 2 * j + 1)
            def _(i):
                unit(2, jnp.minimum(i, j), j - jnp.maximum(i - j, 0))

    rows = lax.broadcasted_iota(jnp.int32, (half, half), 0) + f * half
    cols = lax.broadcasted_iota(jnp.int32, (half, half), 1)
    row_live = rows < live_ref[t]

    @pl.loop(0, 2)
    def _(j):
        self_copy(j).wait_recv()
        keep = row_live & (cols + j * half < live_ref[t]) & (band_ref[t, radius] > 0)
        out_ref[radius, :, columns(j)] = jnp.where(keep, self_local[j] + self_in[j], 0.0)

    def wait_inbox(origin, row, j):
        pltpu.make_async_remote_copy(
            src_ref=outbox.at[0, 0, 0, 0], dst_ref=inbox.at[origin, row, j],
            send_sem=res_send.at[0, 0, 0, 0], recv_sem=res_recv.at[origin, row, j],
            device_id={"freq": 1 - f}, device_id_type=MESH).wait_recv()

    for delta in (1, -1, -2, 2):
        near = t + step * delta
        slot = radius + step * delta
        exists = (r + delta >= 0) & (r + delta < tiles)

        def emit(j, own, near=near, slot=slot, delta=delta):
            wait_inbox(1, ROW[-delta], j)
            total = own + inbox[1, ROW[-delta], j].astype(jnp.float32)
            keep = row_live & (cols + j * half < live_ref[near]) & (band_ref[t, slot] > 0)
            out_ref[slot, :, columns(j)] = jnp.where(keep, total, 0.0)

        def from_inbox(delta=delta, emit=emit):
            @pl.loop(0, 2)
            def _(j):
                wait_inbox(0, ROW[delta], j)
                emit(j, inbox[0, ROW[delta], j].astype(jnp.float32))

        def from_local(delta=delta, emit=emit):
            @pl.loop(0, 2)
            def _(j):
                emit(j, local[delta - 1, j])

        if delta == 2:
            pl.when(exists)(from_local)
        elif delta == 1:
            pl.when(exists & heavy)(from_local)
            pl.when(exists & jnp.logical_not(heavy))(from_inbox)
        else:
            pl.when(exists)(from_inbox)

        @pl.when(jnp.logical_not(exists))
        def _():
            out_ref[slot] = jnp.zeros((half, points), jnp.float32)

    for j in range(2):
        self_copy(j).wait_send()
        for which in range(2):
            @pl.when(jnp.logical_not(heavy))
            def _():
                data_copy(which, j, 1).wait_send()

            @pl.when(r >= 2)
            def _():
                data_copy(which, j, 2).wait_send()

    for k, (first, second) in enumerate(PAIRS):
        made = heavy if second == 1 else (has_far if first == 0 else heavy & has_far)

        @pl.when(made)
        def _():
            @pl.loop(0, 2)
            def _(h):
                for j in range(2):
                    turned_send(k, h, j).wait_send()
                    if first == 0:
                        @pl.when(h != f)
                        def _():
                            plain_send(k, h, j).wait_send()
                    else:
                        plain_send(k, h, j).wait_send()


def per_device(green_recv, green_shot, band_mask, live_counts, freq_bins):
    tiles = lax.axis_size("tile")
    points = green_recv.shape[3]
    slots = band_mask.shape[1]
    half = points // 2
    depth_r = 2 * green_recv.shape[2]
    depth_s = 2 * green_shot.shape[2]
    bf16, f32 = jnp.bfloat16, jnp.float32
    dma = pltpu.SemaphoreType.DMA
    smem = pl.BlockSpec(memory_space=pltpu.SMEM)
    band = pl.pallas_call(
        functools.partial(band_kernel, tiles, slots // 2),
        out_shape=jax.ShapeDtypeStruct((slots, half, points), f32),
        in_specs=[pl.BlockSpec(memory_space=pl.ANY)] * 2 + [smem] * 3,
        out_specs=pl.BlockSpec(memory_space=pltpu.VMEM),
        scratch_shapes=[
            pltpu.VMEM((3, 2, depth_r, half), bf16),
            pltpu.VMEM((3, 2, depth_s, half), bf16),
            pltpu.VMEM((2, 2, points, depth_r), bf16),
            pltpu.VMEM((2, 2, points, depth_s), bf16),
            pltpu.VMEM((2, 2, half, half), f32),
            pltpu.VMEM((2, half, half), f32),
            pltpu.VMEM((2, half, half), f32),
            pltpu.VMEM((2, half, half), f32),
            pltpu.VMEM((3, 2, 2, 2, half, half), bf16),
            pltpu.VMEM((2, 4, 2, half, half), bf16),
            dma((2, 2)),
            dma((2, 2, 2)),
            dma((2, 2, 2)),
            dma((3, 2, 2, 2)),
            dma((2, 4, 2)),
            dma((2,)),
            dma((2,)),
        ],
        compiler_params=pltpu.CompilerParams(
            collective_id=0, has_side_effects=True, vmem_limit_bytes=60 * 1024 * 1024),
    )(green_recv.reshape(depth_r, points), green_shot.reshape(depth_s, points), band_mask, live_counts, freq_bins)
    return jnp.transpose(band, (1, 0, 2))


def solution(mesh):
    return jax.shard_map(
        per_device,
        mesh=mesh,
        in_specs=(
            P(("grp", "freq"), None, None, "tile"),
            P(("grp", "freq"), None, None, "tile"),
            P("grp", None),
            P("grp"),
            P(("grp", "freq")),
        ),
        out_specs=P(("grp", "tile", "freq"), None, None),
        check_vma=False,
    )
```

time: 236 us -> 63.4 us (0.27)
  waiting for transfers between devices: 143 us -> 0 us
  Pallas kernels: 0 us -> 58.4 us
  starting transfers between devices: 44.2 us -> 0 us
  between operations: 16.1 us -> 0.66 us
  other arithmetic: 12.5 us -> 0 us
  local copies, waits for them, and re-layouts: 13.8 us -> 3.62 us
  matrix products: 5.39 us -> 0 us
    ppermute x6 -> x0, waiting for transfers between devices: 110 us -> none  [from_behind(): lax.ppermute(value, axis, [(source, source + steps) for source in range(i...]
    pallas_call x0 -> x1, Pallas kernels: none -> 58.4 us  [per_device(): pl.pallas_call(functools.partial(band_kernel, tiles, slots // 2), out_sha...]
    ppermute x6 -> x0, starting transfers between devices: 44.2 us -> none  [from_behind(): lax.ppermute(value, axis, [(source, source + steps) for source in range(i...]
    psum x1 -> x0, waiting for transfers between devices: 32.3 us -> none  [per_device(): summed_band = lax.psum(local_band, 'freq')]
    another operation x3 -> x0, other arithmetic: 5.43 us -> none  [per_device(): local_band = jnp.stack(blocks, axis=1)]
    dot_general x2 -> x0, matrix products: 5.39 us -> none  [gram_pair(): jnp.einsum('fcri,fdrj->fcidj', left_block, right_block, preferred_element...]
    dynamic_slice x3 -> x0, local copies, waits for them, and re-layouts: 5.11 us -> none  [the longest x1 3.62 us: per_device(): lax.dynamic_slice_in_dim(summed_band, lax.axis_index('freq') * half_rows,...]
    another operation x4 -> x0, local copies, waits for them, and re-layouts: 4.32 us -> none  [the longest x2 4.09 us: per_device(): local_band = jnp.stack(blocks, axis=1)]
  transfers between devices with their start and end apart: 7 -> 0, of which waited for: 4 -> 0; matrix products, arithmetic and copies ran while one was open for 6% -> 0% of each run, Pallas kernels for 0% -> 0%
where the time goes in v1:
time: 63.4 us; the launch traced here: 62.7 us
  Pallas kernels  58.4 us (92%)
  local copies, waits for them, and re-layouts  3.62 us (6%)
  between operations  0.66 us (1%)
    pallas_call x1, Pallas kernels, per_device(): pl.pallas_call(functools.partial(band_kernel, tiles, slots // 2), out_sha...  58.4 us
    unnamed x1, local copies, waits for them, and re-layouts  3.62 us

profile of v1, /device:TPU:13, one launch (start us, length us, event | category | flops | bytes accessed | tf_op | source)
XLA Modules:
  0.0 62.7 jit_solution(18043161630703230392)
XLA Ops:
  0.7 58.4 %shard_map.55 = f32[5,256,512]{2,1,0:T(8,128)} custom-call(bf16[2048,512]{1,0:T(8,128)(2,1)} %bitcast.4, bf16[1024,512]{1,0:T(8,128)(2,1)} %bitcast.5, s32[8,5]{1,0:T(8,128)} %band_ref.1, s32[8]{0:T(128)} %live_ref.1, s32[1]{0:T(128)S(6)} %copy.7.bins_ref), custom_call_target="tpu_custom_call" | custom-call | tf_op jit(solution)/shard_map/pallas_call | solution.py:266
  59.0 3.6 %copy.8 = f32[256,5,512]{2,0,1:T(8,128)} copy(f32[256,5,512]{2,0,1:T(8,128)} %bitcast.3) | data formatting | bytes 5242880

commit v2 on v1

v2 whole, which is shorter than its diff:
```python
import functools

import jax
import jax.numpy as jnp
from jax import lax
from jax.experimental import pallas as pl
from jax.experimental.pallas import tpu as pltpu
from jax.sharding import PartitionSpec as P

BINS = 512
MESH = pl.DeviceIdType.MESH
PAIR = {(1, 0): 0, (2, 0): 1, (2, 1): 2, (1, 2): 2}
ROW = {1: 0, 2: 1, -1: 2, -2: 3}


def band_kernel(tiles, radius, recv_ref, shot_ref, band_ref, live_ref, bins_ref, out_ref,
                far_r, far_s, left_r, left_s, local, self_local, self_out, self_in, outbox, turned, inbox,
                own_sem, data_send, data_recv, res_send, res_recv, self_send, self_recv):
    t = lax.axis_index("tile")
    f = lax.axis_index("freq")
    depth_r, points = recv_ref.shape
    depth_s = shot_ref.shape[0]
    half = points // 2
    part = half // 2
    step = 1 - 2 * f
    r = f * (tiles - 1) + step * t
    heavy = lax.rem(r, 2) == 0
    has_far = r + 2 < tiles
    weight_root = bins_ref[0].astype(jnp.float32) / BINS
    weight = (weight_root * weight_root) * (weight_root * weight_root)

    def columns(j):
        return pl.ds(pl.multiple_of(j * half, half), half)

    def parts(i):
        return pl.ds(pl.multiple_of(i * part, part), part)

    def own_copy(which, j):
        src, dst = ((recv_ref, far_r), (shot_ref, far_s))[which]
        return pltpu.make_async_copy(src.at[:, columns(j)], dst.at[0, j], own_sem.at[which, j])

    def data_copy(which, i, distance):
        src, dst = ((recv_ref, far_r), (shot_ref, far_s))[which]
        return pltpu.make_async_remote_copy(
            src_ref=src.at[:, parts(i)], dst_ref=dst.at[distance, i // 2, :, parts(i % 2)],
            send_sem=data_send.at[which, i, distance - 1], recv_sem=data_recv.at[which, i, distance - 1],
            device_id={"tile": t - step * distance}, device_id_type=MESH)

    for j in range(2):
        for which in range(2):
            own_copy(which, j).start()

    barrier = pltpu.get_barrier_semaphore()
    for distance in range(-2, 3):
        near = t + distance
        for turn in range(2):
            if distance == 0 and turn == 0:
                continue
            other = f if turn == 0 else 1 - f

            @pl.when((near >= 0) & (near < tiles))
            def _():
                pl.semaphore_signal(barrier, inc=1, device_id={"tile": near, "freq": other}, device_id_type=MESH)
    reached = jnp.minimum(t, 2) + jnp.minimum(tiles - 1 - t, 2)
    pl.semaphore_wait(barrier, 2 * reached + 1)

    for i in range(4):
        for which in range(2):
            @pl.when(jnp.logical_not(heavy))
            def _():
                data_copy(which, i, 1).start()

            @pl.when(r >= 2)
            def _():
                data_copy(which, i, 2).start()

    def build_left(slot, i):
        for src, dst, depth in ((far_r, left_r, depth_r // 2), (far_s, left_s, depth_s // 2)):
            re = src[slot, i // 2, 0:depth, parts(i % 2)].T
            im = src[slot, i // 2, depth:2 * depth, parts(i % 2)].T
            dst[slot, i, 0:part, 0:depth] = re
            dst[slot, i, 0:part, depth:2 * depth] = im
            dst[slot, i, part:half, 0:depth] = im
            dst[slot, i, part:half, depth:2 * depth] = -re

    def block(left, i, right, h):
        rr = jnp.dot(left_r[left, i], far_r[right, h], preferred_element_type=jnp.float32)
        ss = jnp.dot(left_s[left, i], far_s[right, h], preferred_element_type=jnp.float32)
        return (rr[:part] * ss[:part] - rr[part:] * ss[part:]) * weight

    def origin_at(h):
        return jnp.where(h == f, 0, 1)

    def plain_send(left, i, right, h, n):
        k, origin, row = PAIR[left, right], origin_at(i // 2), ROW[right - left]
        return pltpu.make_async_remote_copy(
            src_ref=outbox.at[k, n], dst_ref=inbox.at[origin, row, parts(i % 2), columns(h)],
            send_sem=res_send.at[k, 0], recv_sem=res_recv.at[origin, row],
            device_id={"tile": t + step * left, "freq": i // 2}, device_id_type=MESH)

    def turned_send(left, i, right, h, n):
        k, origin, row = PAIR[left, right], origin_at(h), ROW[left - right]
        return pltpu.make_async_remote_copy(
            src_ref=turned.at[k, n], dst_ref=inbox.at[origin, row, :, parts(i)],
            send_sem=res_send.at[k, 1], recv_sem=res_recv.at[origin, row],
            device_id={"tile": t + step * right, "freq": h}, device_id_type=MESH)

    def unit(left, i, right, h, n):
        k = PAIR[left, right]
        value = block(left, i, right, h)
        outbox[k, n] = value.astype(jnp.bfloat16)
        plain_send(left, i, right, h, n).start()
        if right == 0:
            @pl.when(h == f)
            def _():
                local[left - 1, :, parts(i)] = value.T

            @pl.when(h != f)
            def _():
                turned[k, n] = value.T.astype(jnp.bfloat16)
                turned_send(left, i, right, h, n).start()
        else:
            turned[k, n] = value.T.astype(jnp.bfloat16)
            turned_send(left, i, right, h, n).start()

    def self_copy():
        return pltpu.make_async_remote_copy(
            src_ref=self_out, dst_ref=self_in, send_sem=self_send, recv_sem=self_recv,
            device_id={"freq": 1 - f}, device_id_type=MESH)

    for j in range(2):
        for which in range(2):
            own_copy(which, j).wait()

    @pl.loop(0, 4)
    def _(i):
        build_left(0, i)

    for target, dest in ((1 - f, self_out), (f, self_local)):
        @pl.loop(0, 4)
        def _(m):
            dest[parts(m // 2), columns(m % 2)] = block(0, 2 * target + m // 2, 0, m % 2)

        if dest is self_out:
            self_copy().start()

    @pl.loop(0, 4)
    def _(i):
        @pl.when(heavy)
        def _():
            for which in range(2):
                data_copy(which, i, 1).wait_recv()
            build_left(1, i)

            @pl.loop(0, 2)
            def _(h):
                unit(1, i, 0, h, 2 * i + h)

        @pl.when(has_far)
        def _():
            for which in range(2):
                data_copy(which, i, 2).wait_recv()
            build_left(2, i)

            @pl.loop(0, 2)
            def _(h):
                unit(2, i, 0, h, 2 * i + h)

        @pl.when(heavy & has_far)
        def _():
            @pl.loop(0, jnp.where(i == 1, 2, jnp.where(i == 0, 0, 2 * i - 3)))
            def _(m):
                n = jnp.where(i == 1, 2 * m, i + 2 + m)
                unit(2, n // 2, 1, n % 2, n)

            @pl.when(i >= 2)
            def _():
                unit(1, i, 2, 0, 2 * i - 3)

    rows = lax.broadcasted_iota(jnp.int32, (half, half), 0) + f * half
    cols = lax.broadcasted_iota(jnp.int32, (half, half), 1)
    row_live = rows < live_ref[t]

    self_copy().wait_recv()

    @pl.loop(0, 2)
    def _(j):
        keep = row_live & (cols + j * half < live_ref[t]) & (band_ref[t, radius] > 0)
        out_ref[radius, :, columns(j)] = jnp.where(keep, self_local[:, columns(j)] + self_in[:, columns(j)], 0.0)

    def wait_inbox(origin, row):
        pltpu.make_async_remote_copy(
            src_ref=inbox.at[origin, row], dst_ref=inbox.at[origin, row],
            send_sem=res_send.at[0, 0], recv_sem=res_recv.at[origin, row],
            device_id={"freq": 1 - f}, device_id_type=MESH).wait_recv()

    for delta in (1, -1, -2, 2):
        near = t + step * delta
        slot = radius + step * delta
        exists = (r + delta >= 0) & (r + delta < tiles)

        def emit(j, own, near=near, slot=slot, delta=delta):
            total = own + inbox[1, ROW[-delta], :, columns(j)].astype(jnp.float32)
            keep = row_live & (cols + j * half < live_ref[near]) & (band_ref[t, slot] > 0)
            out_ref[slot, :, columns(j)] = jnp.where(keep, total, 0.0)

        def from_inbox(delta=delta, emit=emit):
            wait_inbox(0, ROW[delta])
            wait_inbox(1, ROW[-delta])

            @pl.loop(0, 2)
            def _(j):
                emit(j, inbox[0, ROW[delta], :, columns(j)].astype(jnp.float32))

        def from_local(delta=delta, emit=emit):
            wait_inbox(1, ROW[-delta])

            @pl.loop(0, 2)
            def _(j):
                emit(j, local[delta - 1, :, columns(j)])

        if delta == 2:
            pl.when(exists)(from_local)
        elif delta == 1:
            pl.when(exists & heavy)(from_local)
            pl.when(exists & jnp.logical_not(heavy))(from_inbox)
        else:
            pl.when(exists)(from_inbox)

        @pl.when(jnp.logical_not(exists))
        def _():
            out_ref[slot] = jnp.zeros((half, points), jnp.float32)

    self_copy().wait_send()
    for i in range(4):
        for which in range(2):
            @pl.when(jnp.logical_not(heavy))
            def _():
                data_copy(which, i, 1).wait_send()

            @pl.when(r >= 2)
            def _():
                data_copy(which, i, 2).wait_send()

    def wait_sent(box, sem):
        pltpu.make_async_remote_copy(
            src_ref=box, dst_ref=box, send_sem=sem, recv_sem=res_recv.at[0, 0],
            device_id={"freq": 1 - f}, device_id_type=MESH).wait_send()

    for k, made in enumerate((heavy, has_far, heavy & has_far)):
        @pl.when(made)
        def _():
            wait_sent(outbox.at[k], res_send.at[k, 0])
            wait_sent(turned.at[k] if k == 2 else turned.at[k, 0:4], res_send.at[k, 1])


def per_device(green_recv, green_shot, band_mask, live_counts, freq_bins):
    tiles = lax.axis_size("tile")
    points = green_recv.shape[3]
    slots = band_mask.shape[1]
    half = points // 2
    depth_r = 2 * green_recv.shape[2]
    depth_s = 2 * green_shot.shape[2]
    bf16, f32 = jnp.bfloat16, jnp.float32
    dma = pltpu.SemaphoreType.DMA
    smem = pl.BlockSpec(memory_space=pltpu.SMEM)
    band = pl.pallas_call(
        functools.partial(band_kernel, tiles, slots // 2),
        out_shape=jax.ShapeDtypeStruct((slots, half, points), f32),
        in_specs=[pl.BlockSpec(memory_space=pl.ANY)] * 2 + [smem] * 3,
        out_specs=pl.BlockSpec(memory_space=pltpu.VMEM),
        scratch_shapes=[
            pltpu.VMEM((3, 2, depth_r, half), bf16),
            pltpu.VMEM((3, 2, depth_s, half), bf16),
            pltpu.VMEM((3, 4, half, depth_r), bf16),
            pltpu.VMEM((3, 4, half, depth_s), bf16),
            pltpu.VMEM((2, half, points), f32),
            pltpu.VMEM((half, points), f32),
            pltpu.VMEM((half, points), f32),
            pltpu.VMEM((half, points), f32),
            pltpu.VMEM((3, 8, half // 2, half), bf16),
            pltpu.VMEM((3, 8, half, half // 2), bf16),
            pltpu.VMEM((2, 4, half, points), bf16),
            dma((2, 2)),
            dma((2, 4, 2)),
            dma((2, 4, 2)),
            dma((3, 2)),
            dma((2, 4)),
            dma,
            dma,
        ],
        compiler_params=pltpu.CompilerParams(
            collective_id=0, has_side_effects=True, vmem_limit_bytes=60 * 1024 * 1024),
    )(green_recv.reshape(depth_r, points), green_shot.reshape(depth_s, points), band_mask, live_counts, freq_bins)
    return jnp.transpose(band, (1, 0, 2))


def solution(mesh):
    return jax.shard_map(
        per_device,
        mesh=mesh,
        in_specs=(
            P(("grp", "freq"), None, None, "tile"),
            P(("grp", "freq"), None, None, "tile"),
            P("grp", None),
            P("grp"),
            P(("grp", "freq")),
        ),
        out_specs=P(("grp", "tile", "freq"), None, None),
        check_vma=False,
    )
```

time: 63.4 us -> 61.9 us (0.976)
  Pallas kernels: 58.4 us -> 57.4 us
    pallas_call x1, Pallas kernels: 58.4 us -> 57.4 us  [per_device(): pl.pallas_call(functools.partial(band_kernel, tiles, slots // 2), out_sha...]
where the time goes in v2:
time: 61.9 us; the launch traced here: 61.7 us
  Pallas kernels  57.4 us (93%)
  local copies, waits for them, and re-layouts  3.62 us (6%)
  between operations  0.66 us (1%)
    pallas_call x1, Pallas kernels, per_device(): pl.pallas_call(functools.partial(band_kernel, tiles, slots // 2), out_sha...  57.4 us
    unnamed x1, local copies, waits for them, and re-layouts  3.62 us

profile of v2, /device:TPU:13, one launch (start us, length us, event | category | flops | bytes accessed | tf_op | source)
XLA Modules:
  0.0 61.7 jit_solution(711815911969378573)
XLA Ops:
  0.7 57.4 %shard_map.55 = f32[5,256,512]{2,1,0:T(8,128)} custom-call(bf16[2048,512]{1,0:T(8,128)(2,1)} %bitcast.4, bf16[1024,512]{1,0:T(8,128)(2,1)} %bitcast.5, s32[8,5]{1,0:T(8,128)} %band_ref.1, s32[8]{0:T(128)} %live_ref.1, s32[1]{0:T(128)S(6)} %copy.7.bins_ref), custom_call_target="tpu_custom_call" | custom-call | tf_op jit(solution)/shard_map/pallas_call | solution.py:267
  58.1 3.6 %copy.8 = f32[256,5,512]{2,0,1:T(8,128)} copy(f32[256,5,512]{2,0,1:T(8,128)} %bitcast.3) | data formatting | bytes 5242880

commit v3 on v2

--- a/solution.py
+++ b/solution.py
@@ -8,23 +8,28 @@
 from jax.sharding import PartitionSpec as P
 
 BINS = 512
+VMEM_MIB = 60
 MESH = pl.DeviceIdType.MESH
 PAIR = {(1, 0): 0, (2, 0): 1, (2, 1): 2, (1, 2): 2}
 ROW = {1: 0, 2: 1, -1: 2, -2: 3}
 
 
-def band_kernel(tiles, radius, recv_ref, shot_ref, band_ref, live_ref, bins_ref, out_ref,
-                far_r, far_s, left_r, left_s, local, self_local, self_out, self_in, outbox, turned, inbox,
-                own_sem, data_send, data_recv, res_send, res_recv, self_send, self_recv):
+def place(tiles):
     t = lax.axis_index("tile")
     f = lax.axis_index("freq")
+    step = 1 - 2 * f
+    r = f * (tiles - 1) + step * t
+    return t, f, step, r, lax.rem(r, 2) == 0
+
+
+def band_kernel(tiles, recv_ref, shot_ref, bins_ref, inbox, kept,
+                far_r, far_s, left_r, left_s, own, self_out, self_in, outbox, turned,
+                own_sem, kept_sem, data_send, data_recv, res_send, res_recv, self_send, self_recv):
+    t, f, step, r, heavy = place(tiles)
     depth_r, points = recv_ref.shape
     depth_s = shot_ref.shape[0]
     half = points // 2
     part = half // 2
-    step = 1 - 2 * f
-    r = f * (tiles - 1) + step * t
-    heavy = lax.rem(r, 2) == 0
     has_far = r + 2 < tiles
     weight_root = bins_ref[0].astype(jnp.float32) / BINS
     weight = (weight_root * weight_root) * (weight_root * weight_root)
@@ -45,10 +50,6 @@
             src_ref=src.at[:, parts(i)], dst_ref=dst.at[distance, i // 2, :, parts(i % 2)],
             send_sem=data_send.at[which, i, distance - 1], recv_sem=data_recv.at[which, i, distance - 1],
             device_id={"tile": t - step * distance}, device_id_type=MESH)
-
-    for j in range(2):
-        for which in range(2):
-            own_copy(which, j).start()
 
     barrier = pltpu.get_barrier_semaphore()
     for distance in range(-2, 3):
@@ -62,6 +63,10 @@
             def _():
                 pl.semaphore_signal(barrier, inc=1, device_id={"tile": near, "freq": other}, device_id_type=MESH)
     reached = jnp.minimum(t, 2) + jnp.minimum(tiles - 1 - t, 2)
+    for j in range(2):
+        for which in range(2):
+            own_copy(which, j).start()
+
     pl.semaphore_wait(barrier, 2 * reached + 1)
 
     for i in range(4):
@@ -113,7 +118,7 @@
         if right == 0:
             @pl.when(h == f)
             def _():
-                local[left - 1, :, parts(i)] = value.T
+                own[left, :, parts(i)] = value.T
 
             @pl.when(h != f)
             def _():
@@ -136,7 +141,7 @@
     def _(i):
         build_left(0, i)
 
-    for target, dest in ((1 - f, self_out), (f, self_local)):
+    for target, dest in ((1 - f, self_out), (f, own.at[0])):
         @pl.loop(0, 4)
         def _(m):
             dest[parts(m // 2), columns(m % 2)] = block(0, 2 * target + m // 2, 0, m % 2)
@@ -177,16 +182,10 @@
             def _():
                 unit(1, i, 2, 0, 2 * i - 3)
 
-    rows = lax.broadcasted_iota(jnp.int32, (half, half), 0) + f * half
-    cols = lax.broadcasted_iota(jnp.int32, (half, half), 1)
-    row_live = rows < live_ref[t]
-
     self_copy().wait_recv()
-
-    @pl.loop(0, 2)
-    def _(j):
-        keep = row_live & (cols + j * half < live_ref[t]) & (band_ref[t, radius] > 0)
-        out_ref[radius, :, columns(j)] = jnp.where(keep, self_local[:, columns(j)] + self_in[:, columns(j)], 0.0)
+    own[0] = own[0] + self_in[...]
+    keep_copy = pltpu.make_async_copy(own, kept, kept_sem)
+    keep_copy.start()
 
     def wait_inbox(origin, row):
         pltpu.make_async_remote_copy(
@@ -194,43 +193,16 @@
             send_sem=res_send.at[0, 0], recv_sem=res_recv.at[origin, row],
             device_id={"freq": 1 - f}, device_id_type=MESH).wait_recv()
 
-    for delta in (1, -1, -2, 2):
-        near = t + step * delta
-        slot = radius + step * delta
-        exists = (r + delta >= 0) & (r + delta < tiles)
-
-        def emit(j, own, near=near, slot=slot, delta=delta):
-            total = own + inbox[1, ROW[-delta], :, columns(j)].astype(jnp.float32)
-            keep = row_live & (cols + j * half < live_ref[near]) & (band_ref[t, slot] > 0)
-            out_ref[slot, :, columns(j)] = jnp.where(keep, total, 0.0)
-
-        def from_inbox(delta=delta, emit=emit):
-            wait_inbox(0, ROW[delta])
+    for delta, row in ROW.items():
+        @pl.when((r + delta >= 0) & (r + delta < tiles))
+        def _():
             wait_inbox(1, ROW[-delta])
-
-            @pl.loop(0, 2)
-            def _(j):
-                emit(j, inbox[0, ROW[delta], :, columns(j)].astype(jnp.float32))
-
-        def from_local(delta=delta, emit=emit):
-            wait_inbox(1, ROW[-delta])
-
-            @pl.loop(0, 2)
-            def _(j):
-                emit(j, local[delta - 1, :, columns(j)])
-
-        if delta == 2:
-            pl.when(exists)(from_local)
-        elif delta == 1:
-            pl.when(exists & heavy)(from_local)
-            pl.when(exists & jnp.logical_not(heavy))(from_inbox)
-        else:
-            pl.when(exists)(from_inbox)
-
-        @pl.when(jnp.logical_not(exists))
-        def _():
-            out_ref[slot] = jnp.zeros((half, points), jnp.float32)
-
+            if delta == 1:
+                pl.when(jnp.logical_not(heavy))(lambda: wait_inbox(0, row))
+            elif delta < 0:
+                wait_inbox(0, row)
+
+    keep_copy.wait()
     self_copy().wait_send()
     for i in range(4):
         for which in range(2):
@@ -252,6 +224,70 @@
         def _():
             wait_sent(outbox.at[k], res_send.at[k, 0])
             wait_sent(turned.at[k] if k == 2 else turned.at[k, 0:4], res_send.at[k, 1])
+
+
+def join_kernel(tiles, radius, inbox_ref, kept_ref, band_ref, live_ref, out_ref, inbox, kept, out, inbox_sem, kept_sem, out_sem):
+    t, f, step, r, heavy = place(tiles)
+    _, half, points = kept.shape
+
+    def inbox_copy(origin, row):
+        return pltpu.make_async_copy(inbox_ref.at[origin, row], inbox.at[origin, row], inbox_sem.at[origin, row])
+
+    def kept_copy(k):
+        return pltpu.make_async_copy(kept_ref.at[k], kept.at[k], kept_sem.at[k])
+
+    def out_copy(slot):
+        return pltpu.make_async_copy(out.at[slot], out_ref.at[slot], out_sem.at[slot])
+
+    order = (0, 2, 1, -1, -2)
+    for delta in order:
+        if delta >= 0:
+            kept_copy(delta).start()
+        if delta != 0:
+            inbox_copy(1, ROW[-delta]).start()
+            if delta < 2:
+                inbox_copy(0, ROW[delta]).start()
+    rows = lax.broadcasted_iota(jnp.int32, (half, points), 0) + f * half
+    cols = lax.broadcasted_iota(jnp.int32, (half, points), 1)
+    row_live = rows < live_ref[t]
+    for delta in order:
+        near = t + step * delta
+        slot = radius + step * delta
+        exists = (r + delta >= 0) & (r + delta < tiles)
+        if delta >= 0:
+            kept_copy(delta).wait()
+        if delta != 0:
+            inbox_copy(1, ROW[-delta]).wait()
+            if delta < 2:
+                inbox_copy(0, ROW[delta]).wait()
+
+        def emit(read, near=near, slot=slot):
+            keep = row_live & (cols < live_ref[near]) & (band_ref[t, slot] > 0)
+            out[slot] = jnp.where(keep, read(), 0.0)
+
+        def kept_sum(delta=delta):
+            if delta == 0:
+                return kept[0]
+            return kept[delta] + inbox[1, ROW[-delta]].astype(jnp.float32)
+
+        def inbox_sum(delta=delta):
+            return inbox[0, ROW[delta]].astype(jnp.float32) + inbox[1, ROW[-delta]].astype(jnp.float32)
+
+        if delta in (0, 2):
+            pl.when(exists)(functools.partial(emit, kept_sum))
+        elif delta == 1:
+            pl.when(exists & heavy)(functools.partial(emit, kept_sum))
+            pl.when(exists & jnp.logical_not(heavy))(functools.partial(emit, inbox_sum))
+        else:
+            pl.when(exists)(functools.partial(emit, inbox_sum))
+
+        @pl.when(jnp.logical_not(exists))
+        def _():
+            out[slot] = jnp.zeros((half, points), jnp.float32)
+
+        out_copy(slot).start()
+    for slot in range(2 * radius + 1):
+        out_copy(slot).wait()
 
 
 def per_device(green_recv, green_shot, band_mask, live_counts, freq_bins):
@@ -264,24 +300,27 @@
     bf16, f32 = jnp.bfloat16, jnp.float32
     dma = pltpu.SemaphoreType.DMA
     smem = pl.BlockSpec(memory_space=pltpu.SMEM)
-    band = pl.pallas_call(
-        functools.partial(band_kernel, tiles, slots // 2),
-        out_shape=jax.ShapeDtypeStruct((slots, half, points), f32),
-        in_specs=[pl.BlockSpec(memory_space=pl.ANY)] * 2 + [smem] * 3,
-        out_specs=pl.BlockSpec(memory_space=pltpu.VMEM),
+    anywhere = pl.BlockSpec(memory_space=pl.ANY)
+    inbox, kept = pl.pallas_call(
+        functools.partial(band_kernel, tiles),
+        out_shape=(
+            jax.ShapeDtypeStruct((2, 4, half, points), bf16),
+            jax.ShapeDtypeStruct((3, half, points), f32),
+        ),
+        in_specs=[anywhere, anywhere, smem],
+        out_specs=(anywhere, anywhere),
         scratch_shapes=[
             pltpu.VMEM((3, 2, depth_r, half), bf16),
             pltpu.VMEM((3, 2, depth_s, half), bf16),
             pltpu.VMEM((3, 4, half, depth_r), bf16),
             pltpu.VMEM((3, 4, half, depth_s), bf16),
-            pltpu.VMEM((2, half, points), f32),
-            pltpu.VMEM((half, points), f32),
+            pltpu.VMEM((3, half, points), f32),
             pltpu.VMEM((half, points), f32),
             pltpu.VMEM((half, points), f32),
             pltpu.VMEM((3, 8, half // 2, half), bf16),
             pltpu.VMEM((3, 8, half, half // 2), bf16),
-            pltpu.VMEM((2, 4, half, points), bf16),
             dma((2, 2)),
+            dma,
             dma((2, 4, 2)),
             dma((2, 4, 2)),
             dma((3, 2)),
@@ -290,8 +329,23 @@
             dma,
         ],
         compiler_params=pltpu.CompilerParams(
-            collective_id=0, has_side_effects=True, vmem_limit_bytes=60 * 1024 * 1024),
-    )(green_recv.reshape(depth_r, points), green_shot.reshape(depth_s, points), band_mask, live_counts, freq_bins)
+            collective_id=0, has_side_effects=True, vmem_limit_bytes=VMEM_MIB * 1024 * 1024),
+    )(green_recv.reshape(depth_r, points), green_shot.reshape(depth_s, points), freq_bins)
+    band = pl.pallas_call(
+        functools.partial(join_kernel, tiles, slots // 2),
+        out_shape=jax.ShapeDtypeStruct((slots, half, points), f32),
+        in_specs=[anywhere, anywhere, smem, smem],
+        out_specs=anywhere,
+        scratch_shapes=[
+            pltpu.VMEM((2, 4, half, points), bf16),
+            pltpu.VMEM((3, half, points), f32),
+            pltpu.VMEM((slots, half, points), f32),
+            dma((2, 4)),
+            dma((3,)),
+            dma((slots,)),
+        ],
+        compiler_params=pltpu.CompilerParams(vmem_limit_bytes=VMEM_MIB * 1024 * 1024),
+    )(inbox, kept, band_mask, live_counts)
     return jnp.transpose(band, (1, 0, 2))
 
 

time: 61.9 us -> 59.7 us (0.964)
  local copies, waits for them, and re-layouts: 3.62 us -> 0 us
  Pallas kernels: 57.4 us -> 58.9 us
    unnamed x1 -> x0, local copies, waits for them, and re-layouts: 3.62 us -> none
    pallas_call x1 -> x2, Pallas kernels: 57.4 us -> 58.9 us  [the longest x1 54.9 us: per_device(): pl.pallas_call(functools.partial(band_kernel, tiles), out_shape=(jax.Shap...]
where the time goes in v3:
time: 59.7 us; the launch traced here: 59.6 us
  Pallas kernels  58.9 us (99%)
  between operations  0.66 us (1%)
    pallas_call x1, Pallas kernels, per_device(): pl.pallas_call(functools.partial(band_kernel, tiles), out_shape=(jax.Shap...  54.9 us
    pallas_call x1, Pallas kernels, per_device(): pl.pallas_call(functools.partial(join_kernel, tiles, slots // 2), out_sha...  3.95 us

profile of v3, /device:TPU:13, one launch (start us, length us, event | category | flops | bytes accessed | tf_op | source)
XLA Modules:
  0.0 59.6 jit_solution(7519478133364326625)
XLA Ops:
  0.7 54.9 %shard_map.55 = (bf16[2,4,256,512]{3,2,1,0:T(8,128)(2,1)}, f32[3,256,512]{2,1,0:T(8,128)}) custom-call(bf16[2048,512]{1,0:T(8,128)(2,1)} %bitcast.3, bf16[1024,512]{1,0:T(8,128)(2,1)} %bitcast.4, s32[1]{0:T(128)S(6)} %copy.6.bins_ref), custom_call_target="tpu_custom_call" | custom-call | tf_op jit(solution)/shard_map/pallas_call | solution.py:304
  55.6 4.0 %shard_map.56 = f32[5,256,512]{2,1,0:T(8,128)} custom-call(bf16[2,4,256,512]{3,2,1,0:T(8,128)(2,1)} %get-tuple-element.7.inbox_ref, f32[3,256,512]{2,1,0:T(8,128)} %get-tuple-element.8.kept_ref, s32[8,5]{1,0:T(8,128)} %band_ref.1, s32[8]{0:T(128)} %live_ref.1), custom_call_target="tpu_custom_call" | custom-call | tf_op jit(solution)/shard_map/pallas_call | solution.py:334

commit v4 on v3

--- a/solution.py
+++ b/solution.py
@@ -161,6 +161,10 @@
             def _(h):
                 unit(1, i, 0, h, 2 * i + h)
 
+        @pl.when(heavy & has_far & (i >= 2))
+        def _():
+            unit(1, i, 2, 0, 2 * i - 3)
+
         @pl.when(has_far)
         def _():
             for which in range(2):
@@ -177,10 +181,6 @@
             def _(m):
                 n = jnp.where(i == 1, 2 * m, i + 2 + m)
                 unit(2, n // 2, 1, n % 2, n)
-
-            @pl.when(i >= 2)
-            def _():
-                unit(1, i, 2, 0, 2 * i - 3)
 
     self_copy().wait_recv()
     own[0] = own[0] + self_in[...]
@@ -241,12 +241,15 @@
 
     order = (0, 2, 1, -1, -2)
     for delta in order:
-        if delta >= 0:
+        if delta == 1:
+            pl.when(heavy)(kept_copy(1).start)
+            pl.when(jnp.logical_not(heavy))(inbox_copy(0, ROW[1]).start)
+        elif delta >= 0:
             kept_copy(delta).start()
+        else:
+            inbox_copy(0, ROW[delta]).start()
         if delta != 0:
             inbox_copy(1, ROW[-delta]).start()
-            if delta < 2:
-                inbox_copy(0, ROW[delta]).start()
     rows = lax.broadcasted_iota(jnp.int32, (half, points), 0) + f * half
     cols = lax.broadcasted_iota(jnp.int32, (half, points), 1)
     row_live = rows < live_ref[t]
@@ -254,12 +257,15 @@
         near = t + step * delta
         slot = radius + step * delta
         exists = (r + delta >= 0) & (r + delta < tiles)
-        if delta >= 0:
+        if delta == 1:
+            pl.when(heavy)(kept_copy(1).wait)
+            pl.when(jnp.logical_not(heavy))(inbox_copy(0, ROW[1]).wait)
+        elif delta >= 0:
             kept_copy(delta).wait()
+        else:
+            inbox_copy(0, ROW[delta]).wait()
         if delta != 0:
             inbox_copy(1, ROW[-delta]).wait()
-            if delta < 2:
-                inbox_copy(0, ROW[delta]).wait()
 
         def emit(read, near=near, slot=slot):
             keep = row_live & (cols < live_ref[near]) & (band_ref[t, slot] > 0)

time: 59.7 us -> 59.6 us (level)
  no operation moved by 1% of the time
where the time goes in v4:
time: 59.6 us; the launch traced here: 59.4 us
  Pallas kernels  58.8 us (99%)
  between operations  0.66 us (1%)
    pallas_call x1, Pallas kernels, per_device(): pl.pallas_call(functools.partial(band_kernel, tiles), out_shape=(jax.Shap...  54.9 us
    pallas_call x1, Pallas kernels, per_device(): pl.pallas_call(functools.partial(join_kernel, tiles, slots // 2), out_sha...  3.87 us

profile of v4, /device:TPU:13, one launch (start us, length us, event | category | flops | bytes accessed | tf_op | source)
XLA Modules:
  0.0 59.4 jit_solution(10419763902278982355)
XLA Ops:
  0.7 54.9 %shard_map.55 = (bf16[2,4,256,512]{3,2,1,0:T(8,128)(2,1)}, f32[3,256,512]{2,1,0:T(8,128)}) custom-call(bf16[2048,512]{1,0:T(8,128)(2,1)} %bitcast.3, bf16[1024,512]{1,0:T(8,128)(2,1)} %bitcast.4, s32[1]{0:T(128)S(6)} %copy.6.bins_ref), custom_call_target="tpu_custom_call" | custom-call | tf_op jit(solution)/shard_map/pallas_call | solution.py:310
  55.5 3.9 %shard_map.56 = f32[5,256,512]{2,1,0:T(8,128)} custom-call(bf16[2,4,256,512]{3,2,1,0:T(8,128)(2,1)} %get-tuple-element.7.inbox_ref, f32[3,256,512]{2,1,0:T(8,128)} %get-tuple-element.8.kept_ref, s32[8,5]{1,0:T(8,128)} %band_ref.1, s32[8]{0:T(128)} %live_ref.1), custom_call_target="tpu_custom_call" | custom-call | tf_op jit(solution)/shard_map/pallas_call | solution.py:340
